TPU v7x, 256 devices: a whole 4x4x8 slice. The times are simulated.
256 devices in a mesh: seq: 32 (over x, z), tp: 8 (over y, core).
Axes of the slice: x: 4, y: 4, z: 8, core: 2. Of those that a mesh axis runs over, the one named last changes fastest.
Arguments:
- event_vectors: bfloat16 [16384, 6144], P('seq'), may hold values from -6 to 6
- question_projector: bfloat16 [6144, 4096], P('seq', 'tp'), may hold values from -0.078125 to 0.078125
- lookup_projector: bfloat16 [6144, 4096], P('seq', 'tp'), may hold values from -0.078125 to 0.078125
- content_projector: bfloat16 [6144, 4096], P('seq', 'tp'), may hold values from -0.078125 to 0.078125
- channel_fading_speed: float32 [32], P('tp'), may hold values from 1.2207031e-05 to 0.03334
- surge_fading: float32 [16384], P('seq'), may hold values from -0.6932 to 0, as said below
- channel_scaling_coefficient: float32 [4096], P('tp'), may hold values from 0.1 to 1.9
- final_projector: bfloat16 [4096, 6144], P('seq', 'tp'), may hold values from -0.09375 to 0.09375
Outputs:
- mixed: bfloat16 [16384, 6144], P('seq', 'tp')
Inputs may be any that keep to these rules, and one draw needn't show every extreme that they name: `surge_fading`: zero at all but a few positions of the sequence.
All inputs are finite; a program needn't handle non-finite values.
Results may differ from a plain program's by a relative error of at most 0.0063.
Values may be sent and summed in bfloat16 or wider, within the bound.
A program may use at most 128 MiB of HBM per device.

v0:
```python
import jax
import jax.numpy as jnp
from jax import lax
from jax.sharding import PartitionSpec as P

HD = 128
SPAN_LENGTH = 512


def entering(part, axis, combine, identity):
    place = lax.axis_index(axis)
    gathered = jax.tree.map(lambda a: lax.all_gather(a, axis), part)
    state = jax.tree.map(lambda a, e: jnp.zeros_like(a) + jnp.asarray(e, a.dtype), part, identity)

    def one(step, state):
        return combine(
            state, jax.tree.map(lambda a: lax.dynamic_index_in_dim(a, step, 0, False), gathered)
        )

    return lax.fori_loop(0, place, one, state)


def block_pass(carry, inputs):
    carried, before = carry
    query_block, key_block, value_block, log_block = inputs
    inside = jnp.cumsum(log_block, axis=0)
    block_total = inside[-1]
    highest = lax.Precision.HIGHEST
    scores = jnp.einsum("thd,shd->hts", query_block, key_block, precision=highest)
    spread_log = inside.T[:, :, None] - inside.T[:, None, :]
    rows_index = lax.broadcasted_iota(jnp.int32, (SPAN_LENGTH, SPAN_LENGTH), 0)
    cols_index = lax.broadcasted_iota(jnp.int32, (SPAN_LENGTH, SPAN_LENGTH), 1)
    causal = (rows_index >= cols_index)[None, :, :]
    weight = jnp.where(causal, jnp.exp(jnp.where(causal, spread_log, 0.0)), 0.0)
    within = jnp.einsum("hts,shd->thd", scores * weight, value_block, precision=highest)
    across = jnp.einsum(
        "thd,hde->the", query_block * jnp.exp(inside)[:, :, None], carried, precision=highest
    )
    updated = jnp.exp(block_total)[:, None, None] * carried + jnp.einsum(
        "shd,she->hde",
        key_block * jnp.exp(block_total[None, :] - inside)[:, :, None],
        value_block,
        precision=highest,
    )
    factor = jnp.exp(before[None, :] + inside)
    return ((updated, before + block_total), (within + across, factor))


def chain_combine(earlier, later):
    return (earlier[0] + later[0], jnp.exp(later[0])[:, None, None] * earlier[1] + later[1])


def local(
    event_vectors,
    question_projector,
    lookup_projector,
    content_projector,
    channel_fading_speed,
    surge_fading,
    channel_scaling_coefficient,
    final_projector,
):
    tok_count = event_vectors.shape[0]
    number_of_heads = channel_fading_speed.shape[0]

    def project_rows(shard_rows):
        return jnp.dot(event_vectors, shard_rows, preferred_element_type=jnp.float32)

    query_sum = project_rows(lax.all_gather(question_projector, "seq", axis=0, tiled=True))
    key_sum = project_rows(lax.all_gather(lookup_projector, "seq", axis=0, tiled=True))
    value_sum = project_rows(lax.all_gather(content_projector, "seq", axis=0, tiled=True))
    queries = jax.nn.silu(query_sum).astype(jnp.bfloat16)
    keys_act = jax.nn.silu(key_sum).astype(jnp.bfloat16)
    values_act = value_sum.astype(jnp.bfloat16)
    span_count = tok_count // SPAN_LENGTH
    shaped = (span_count, SPAN_LENGTH, number_of_heads, HD)
    query_blocks = queries.astype(jnp.float32).reshape(shaped)
    key_blocks = keys_act.astype(jnp.float32).reshape(shaped)
    value_blocks = values_act.astype(jnp.float32).reshape(shaped)
    stepwise_fading_exponent = (surge_fading[:, None] - channel_fading_speed[None, :]).reshape(
        (span_count, SPAN_LENGTH, number_of_heads)
    )
    start = (
        jnp.zeros((number_of_heads, HD, HD), jnp.float32),
        jnp.zeros((number_of_heads,), jnp.float32),
    )
    (local_state, local_log), (outputs, factors) = lax.scan(
        block_pass, start, (query_blocks, key_blocks, value_blocks, stepwise_fading_exponent)
    )
    identity = (
        jnp.zeros((number_of_heads,), jnp.float32),
        jnp.zeros((number_of_heads, HD, HD), jnp.float32),
    )
    prior_log, incoming = entering((local_log, local_state), "seq", chain_combine, identity)
    query_flat = query_blocks.reshape((tok_count, number_of_heads, HD))
    reached = jnp.einsum("thd,hde->the", query_flat, incoming, precision=lax.Precision.HIGHEST)
    attention = (
        outputs.reshape((tok_count, number_of_heads, HD))
        + factors.reshape((tok_count, number_of_heads))[:, :, None] * reached
    )
    meansq = jnp.mean(attention * attention, axis=-1, keepdims=True)
    normed = (
        attention
        / jnp.sqrt(meansq + 1e-05)
        * channel_scaling_coefficient.reshape((number_of_heads, HD))[None, :, :]
    )
    normed = normed.reshape((tok_count, number_of_heads * HD)).astype(jnp.bfloat16)
    every_head = lax.all_gather(normed, "tp", axis=1, tiled=True)
    mixed = jnp.dot(
        every_head,
        lax.all_gather(final_projector, "seq", axis=0, tiled=True),
        preferred_element_type=jnp.float32,
    )
    return mixed.astype(jnp.bfloat16)


def solution(mesh):
    in_specs = (
        P("seq", None),
        P("seq", "tp"),
        P("seq", "tp"),
        P("seq", "tp"),
        P("tp"),
        P("seq"),
        P("tp"),
        P("seq", "tp"),
    )
    out_specs = P("seq", "tp")
    return jax.shard_map(local, mesh=mesh, in_specs=in_specs, out_specs=out_specs, check_vma=False)
```

profile of v0, /device:TPU:1, one launch (start us, length us, event | category | flops | bytes accessed | tf_op | source)
XLA Modules:
  0.0 514.1 jit_solution(17631043664003188020)
XLA Ops:
  6.5 0.7 all-gather.9.cloned.1.call-update
  7.3 0.7 all-gather.13.cloned.1.call-update
  8.1 0.7 all-gather.11.cloned.1.call-update
  8.8 0.8 broadcast_subtract_fusion
  9.6 1.2 reduce-window.6
  11.5 90.6 %all-gather.9.cloned.1.call-done = bf16[6144,512]{1,0:T(8,128)(2,1)} async-done(((bf16[192,512]{1,0:T(8,128)(2,1)}), bf16[6144,512]{1,0:T(8,128)(2,1)}) %all-gather.9.cloned.1.call-update) | async-done | bytes 6291472 | tf_op jit(solution)/shard_map/all_gather | solution.py:71
  102.1 8.1 %convolution_convert_fusion.1 = bf16[512,512]{0,1:T(8,128)(2,1)S(1)} fusion(bf16[512,6144]{1,0:T(8,128)(2,1)} %param.10, bf16[6144,512]{1,0:T(8,128)(2,1)} %all-gather.9.cloned.1.call-done), kind=kOutput, calls=%fused_computation.18 | convolution fusion | flops 3221487616 | bytes 13107200 | tf_op jit(solution)/shard_map/dot_general | solution.py:67
  110.2 80.2 %all-gather.13.cloned.1.call-done = bf16[6144,512]{1,0:T(8,128)(2,1)} async-done(((bf16[192,512]{1,0:T(8,128)(2,1)}), bf16[6144,512]{1,0:T(8,128)(2,1)}) %all-gather.13.cloned.1.call-update) | async-done | bytes 6291472 | tf_op jit(solution)/shard_map/all_gather | solution.py:70
  190.4 8.2 %multiply_convert_fusion.1 = bf16[512,512]{0,1:T(8,128)(2,1)S(1)} fusion(bf16[512,6144]{1,0:T(8,128)(2,1)} %param.10, bf16[6144,512]{1,0:T(8,128)(2,1)} %all-gather.13.cloned.1.call-done), kind=kOutput, calls=%fused_computation.27 | convolution fusion | flops 3222536192 | bytes 13107200 | tf_op jit(solution)/shard_map/dot_general | solution.py:67
  198.6 1.4 convolution_add_fusion.1
  200.0 0.5 all-gather.17.cloned.1.call-update
  200.6 31.6 %all-gather.1 = f32[32,1,4]{2,1,0:T(1,128)S(1)} all-gather(f32[1,1,4]{2,1,0:T(1,128)S(1)} %bitcast.69), channel_id=1, replica_groups=mesh['seq'=32,'tp'=8] {'seq'}, dimensions={0}, use_global_device_ids=true | all-gather | bytes 528 | tf_op jit(solution)/shard_map/all_gather | solution.py:12
  232.3 46.4 %all-gather.11.cloned.1.call-done = bf16[6144,512]{1,0:T(8,128)(2,1)} async-done(((bf16[192,512]{1,0:T(8,128)(2,1)}), bf16[6144,512]{1,0:T(8,128)(2,1)}) %all-gather.11.cloned.1.call-update) | async-done | bytes 6291472 | tf_op jit(solution)/shard_map/all_gather | solution.py:69
  278.7 8.2 %multiply_convert_fusion.2 = bf16[512,512]{0,1:T(8,128)(2,1)S(1)} fusion(bf16[512,6144]{1,0:T(8,128)(2,1)} %param.10, bf16[6144,512]{1,0:T(8,128)(2,1)} %all-gather.11.cloned.1.call-done), kind=kOutput, calls=%fused_computation.28 | convolution fusion | flops 3222536192 | bytes 13107200 | tf_op jit(solution)/shard_map/dot_general | solution.py:67
  286.9 0.7 fusion.23
  287.6 3.7 fusion
  291.3 1.0 fusion.12
  292.4 84.0 %all-gather.19.cloned.1.call-done = f32[128,128,128]{2,1,0:T(8,128)} async-done(((f32[4,128,128]{2,1,0:T(8,128)}), f32[128,128,128]{2,1,0:T(8,128)}) %all-gather.19.cloned.1.call-update) | async-done | bytes 8388624 | tf_op jit(solution)/shard_map/all_gather | solution.py:12
  376.4 0.2 while.3
  376.6 0.7 multiply_reduce_fusion
  377.4 0.9 multiply_convert_fusion
  378.4 86.3 %all-gather.17.cloned.1.call-done = bf16[4096,768]{1,0:T(8,128)(2,1)} async-done(((bf16[128,768]{1,0:T(8,128)(2,1)}), bf16[4096,768]{1,0:T(8,128)(2,1)}) %all-gather.17.cloned.1.call-update) | async-done | bytes 6291472 | tf_op jit(solution)/shard_map/all_gather | solution.py:111
  464.6 34.2 %all-gather.15.cloned.1.call-done = bf16[512,4096]{0,1:T(8,128)(2,1)} async-done(((bf16[512,512]{0,1:T(8,128)(2,1)}), bf16[512,4096]{0,1:T(8,128)(2,1)}) %all-gather.15.cloned.1.call-update) | async-done | bytes 4194320 | tf_op jit(solution)/shard_map/all_gather | solution.py:108
  498.8 8.4 %convolution_convert_fusion = bf16[512,768]{1,0:T(8,128)(2,1)} fusion(bf16[512,4096]{0,1:T(8,128)(2,1)} %all-gather.15.cloned.1.call-done, bf16[4096,768]{1,0:T(8,128)(2,1)} %all-gather.17.cloned.1.call-done), kind=kOutput, calls=%fused_computation.12 | convolution fusion | flops 3221618688 | bytes 11272192 | tf_op jit(solution)/shard_map/dot_general | solution.py:109
  (20 shorter events, 1.0 us)
Async XLA Ops:
  6.5 95.6 %all-gather.9.cloned.1.call-start = ((), (), s32[]{:S(2)}) async-start(), calls=%async_computation | async-start | bytes 6488064 | tf_op jit(solution)/shard_map/all_gather | solution.py:71
  7.3 183.1 %all-gather.13.cloned.1.call-start = ((), (), s32[]{:S(2)}) async-start(), calls=%async_computation.2 | async-start | bytes 6488064 | tf_op jit(solution)/shard_map/all_gather | solution.py:70
  8.0 270.7 %all-gather.11.cloned.1.call-start = ((), (), s32[]{:S(2)}) async-start(), calls=%async_computation.1 | async-start | bytes 6488064 | tf_op jit(solution)/shard_map/all_gather | solution.py:69
  8.7 367.6 %all-gather.19.cloned.1.call-start = ((), (), s32[]{:S(2)}) async-start(), calls=%async_computation.5 | async-start | bytes 8650752 | tf_op jit(solution)/shard_map/all_gather | solution.py:12
  200.0 264.7 %all-gather.17.cloned.1.call-start = ((), (), s32[]{:S(2)}) async-start(), calls=%async_computation.4 | async-start | bytes 6488064 | tf_op jit(solution)/shard_map/all_gather | solution.py:111
  200.6 298.3 %all-gather.15.cloned.1.call-start = ((), (), s32[]{:S(2)}) async-start(), calls=%async_computation.3 | async-start | bytes 4718592 | tf_op jit(solution)/shard_map/all_gather | solution.py:108
  291.3 86.1 %copy-start = (f32[512]{0:T(512)S(1)}, f32[512]{0:T(512)}, u32[]{:S(2)}) copy-start(f32[512]{0:T(512)} %param.16) | copy-start | bytes 6148
Sparse Core Ops, SparseCore 0:
  9.9 92.1 all-gather.8
  104.7 85.6 all-gather.12
  192.9 85.6 all-gather.10
  281.1 95.1 all-gather.18
  378.8 85.8 all-gather.16
  466.3 32.4 all-gather.14
where the time goes:
time: 515 us; the launch traced here: 514 us
  waiting for transfers between devices  424 us (82%)
  matrix products  40.4 us (8%)
  blocking collectives  31.6 us (6%)
  between operations  13.6 us (3%)
    all_gather x1, waiting for transfers between devices, local(): lax.all_gather(content_projector, 'seq', axis=0, tiled=True)  90.6 us
    all_gather x1, waiting for transfers between devices, local(): lax.all_gather(final_projector, 'seq', axis=0, tiled=True)  86.3 us
    all_gather x1, waiting for transfers between devices, entering(): gathered = jax.tree.map(lambda a: lax.all_gather(a, axis), part)  84 us
    all_gather x1, waiting for transfers between devices, local(): lax.all_gather(lookup_projector, 'seq', axis=0, tiled=True)  80.2 us
    all_gather x1, waiting for transfers between devices, local(): lax.all_gather(question_projector, 'seq', axis=0, tiled=True)  46.4 us
    all_gather x1, waiting for transfers between devices, local(): every_head = lax.all_gather(normed, 'tp', axis=1, tiled=True)  34.2 us
    all_gather x1, blocking collectives, entering(): gathered = jax.tree.map(lambda a: lax.all_gather(a, axis), part)  31.6 us
    dot_general x3, matrix products, project_rows(): jnp.dot(event_vectors, shard_rows, preferred_element_type=jnp.float32)  24.4 us
  transfers between devices with their start and end apart: 6, of which 6 were waited for; matrix products, arithmetic and copies ran while one was open for 7% of the time, Pallas kernels for 0%

commit v1 on v0

--- a/solution.py
+++ b/solution.py
@@ -105,7 +105,24 @@
         * channel_scaling_coefficient.reshape((number_of_heads, HD))[None, :, :]
     )
     normed = normed.reshape((tok_count, number_of_heads * HD)).astype(jnp.bfloat16)
-    every_head = lax.all_gather(normed, "tp", axis=1, tiled=True)
+    size, place_2, span = (lax.axis_size("tp"), lax.axis_index("tp"), normed.shape[1])
+    right = [(i, (i + 1) % size) for i in range(size)]
+    left = [(i, (i - 1) % size) for i in range(size)]
+    whole = jnp.zeros((*normed.shape[:1], size * span, *normed.shape[1 + 1 :]), normed.dtype)
+    whole = lax.dynamic_update_slice_in_dim(whole, normed, place_2 * span, axis=1)
+    from_left = from_right = normed
+    halfway = size // 2
+    for step_2 in range(1, halfway + 1):
+        from_left = lax.ppermute(from_left, "tp", right)
+        whole = lax.dynamic_update_slice_in_dim(
+            whole, from_left, (place_2 - step_2) % size * span, axis=1
+        )
+        if step_2 < size - halfway:
+            from_right = lax.ppermute(from_right, "tp", left)
+            whole = lax.dynamic_update_slice_in_dim(
+                whole, from_right, (place_2 + step_2) % size * span, axis=1
+            )
+    every_head = whole
     mixed = jnp.dot(
         every_head,
         lax.all_gather(final_projector, "seq", axis=0, tiled=True),

time: 515 us -> 481 us (0.934)
  waiting for transfers between devices: 424 us -> 371 us
  starting transfers between devices: 0.2 us -> 11.3 us
  local copies, waits for them, and re-layouts: 0.37 us -> 9.27 us
    all_gather x1 -> x0, waiting for transfers between devices: 34.2 us -> none  [local(): every_head = lax.all_gather(normed, 'tp', axis=1, tiled=True)]
    all_gather x1, waiting for transfers between devices: 86.3 us -> 52.1 us  [local(): lax.all_gather(final_projector, 'seq', axis=0, tiled=True)]
    ppermute x0 -> x7, waiting for transfers between devices: none -> 15 us  [the longest x4 14.9 us: local(): from_left = lax.ppermute(from_left, 'tp', right)]
    ppermute x0 -> x7, starting transfers between devices: none -> 11.1 us  [the longest x4 9.63 us: local(): from_left = lax.ppermute(from_left, 'tp', right)]
    dynamic_update_slice x0 -> x8, local copies, waits for them, and re-layouts: none -> 6.66 us  [the longest x4 3.34 us: local(): lax.dynamic_update_slice_in_dim(whole, from_left, (place_2 - step_2) % si...]
  transfers between devices with their start and end apart: 6 -> 12, of which waited for: 6 -> 10; matrix products, arithmetic and copies ran while one was open for 7% -> 9% of each run, Pallas kernels for 0% -> 0%
where the time goes in v1:
time: 481 us; the launch traced here: 480 us
  waiting for transfers between devices  371 us (77%)
  matrix products  40.4 us (8%)
  blocking collectives  31.6 us (7%)
  between operations  13.3 us (3%)
  starting transfers between devices  11.3 us (2%)
  local copies, waits for them, and re-layouts  9.27 us (2%)
    all_gather x1, waiting for transfers between devices, local(): lax.all_gather(content_projector, 'seq', axis=0, tiled=True)  90.6 us
    all_gather x1, waiting for transfers between devices, entering(): gathered = jax.tree.map(lambda a: lax.all_gather(a, axis), part)  84 us
    all_gather x1, waiting for transfers between devices, local(): lax.all_gather(lookup_projector, 'seq', axis=0, tiled=True)  80.2 us
    all_gather x1, waiting for transfers between devices, local(): lax.all_gather(final_projector, 'seq', axis=0, tiled=True)  52.1 us
    all_gather x1, waiting for transfers between devices, local(): lax.all_gather(question_projector, 'seq', axis=0, tiled=True)  46.4 us
    all_gather x1, blocking collectives, entering(): gathered = jax.tree.map(lambda a: lax.all_gather(a, axis), part)  31.6 us
    dot_general x3, matrix products, project_rows(): jnp.dot(event_vectors, shard_rows, preferred_element_type=jnp.float32)  24.4 us
    ppermute x4, waiting for transfers between devices, local(): from_left = lax.ppermute(from_left, 'tp', right)  14.9 us
  transfers between devices with their start and end apart: 12, of which 10 were waited for; matrix products, arithmetic and copies ran while one was open for 9% of the time, Pallas kernels for 0%

profile of v1, /device:TPU:1, one launch (start us, length us, event | category | flops | bytes accessed | tf_op | source)
XLA Modules:
  0.0 479.6 jit_solution(6585737655859538075)
XLA Ops:
  9.6 1.2 reduce-window.6
  11.5 90.6 %all-gather.8.cloned.1.call-done = bf16[6144,512]{1,0:T(8,128)(2,1)} async-done(((bf16[192,512]{1,0:T(8,128)(2,1)}), bf16[6144,512]{1,0:T(8,128)(2,1)}) %all-gather.8.cloned.1.call-update) | async-done | bytes 6291472 | tf_op jit(solution)/shard_map/all_gather | solution.py:71
  102.1 8.1 %convolution_convert_fusion.1 = bf16[512,512]{0,1:T(8,128)(2,1)S(1)} fusion(bf16[512,6144]{1,0:T(8,128)(2,1)} %param.10, bf16[6144,512]{1,0:T(8,128)(2,1)} %all-gather.8.cloned.1.call-done), kind=kOutput, calls=%fused_computation.18 | convolution fusion | flops 3221487616 | bytes 13107200 | tf_op jit(solution)/shard_map/dot_general | solution.py:67
  110.2 80.2 %all-gather.12.cloned.1.call-done = bf16[6144,512]{1,0:T(8,128)(2,1)} async-done(((bf16[192,512]{1,0:T(8,128)(2,1)}), bf16[6144,512]{1,0:T(8,128)(2,1)}) %all-gather.12.cloned.1.call-update) | async-done | bytes 6291472 | tf_op jit(solution)/shard_map/all_gather | solution.py:70
  190.4 8.2 %multiply_convert_fusion.1 = bf16[512,512]{0,1:T(8,128)(2,1)S(1)} fusion(bf16[512,6144]{1,0:T(8,128)(2,1)} %param.10, bf16[6144,512]{1,0:T(8,128)(2,1)} %all-gather.12.cloned.1.call-done), kind=kOutput, calls=%fused_computation.27 | convolution fusion | flops 3222536192 | bytes 13107200 | tf_op jit(solution)/shard_map/dot_general | solution.py:67
  198.6 1.4 convolution_add_fusion.1
  200.6 31.6 %all-gather.1 = f32[32,1,4]{2,1,0:T(1,128)S(1)} all-gather(f32[1,1,4]{2,1,0:T(1,128)S(1)} %bitcast.71), channel_id=1, replica_groups=mesh['seq'=32,'tp'=8] {'seq'}, dimensions={0}, use_global_device_ids=true | all-gather | bytes 528 | tf_op jit(solution)/shard_map/all_gather | solution.py:12
  232.3 46.4 %all-gather.10.cloned.1.call-done = bf16[6144,512]{1,0:T(8,128)(2,1)} async-done(((bf16[192,512]{1,0:T(8,128)(2,1)}), bf16[6144,512]{1,0:T(8,128)(2,1)}) %all-gather.10.cloned.1.call-update) | async-done | bytes 6291472 | tf_op jit(solution)/shard_map/all_gather | solution.py:69
  278.7 8.2 %multiply_convert_fusion.2 = bf16[512,512]{0,1:T(8,128)(2,1)S(1)} fusion(bf16[512,6144]{1,0:T(8,128)(2,1)} %param.10, bf16[6144,512]{1,0:T(8,128)(2,1)} %all-gather.10.cloned.1.call-done), kind=kOutput, calls=%fused_computation.28 | convolution fusion | flops 3222536192 | bytes 13107200 | tf_op jit(solution)/shard_map/dot_general | solution.py:67
  287.6 3.7 fusion
  291.3 1.0 fusion.12
  292.4 84.0 %all-gather.16.cloned.1.call-done = f32[128,128,128]{2,1,0:T(8,128)} async-done(((f32[4,128,128]{2,1,0:T(8,128)}), f32[128,128,128]{2,1,0:T(8,128)}) %all-gather.16.cloned.1.call-update) | async-done | bytes 8388624 | tf_op jit(solution)/shard_map/all_gather | solution.py:12
  377.5 2.2 collective-permute-start
  379.7 6.1 %collective-permute-done = bf16[512,512]{0,1:T(8,128)(2,1)S(1)} collective-permute-done((bf16[512,512]{0,1:T(8,128)(2,1)S(1)}, bf16[512,512]{0,1:T(8,128)(2,1)S(1)}, u32[]{:S(2)}, u32[]{:S(2)}) %collective-permute-start) | collective-permute-done | bytes 524320 | tf_op jit(solution)/shard_map/ppermute | solution.py:116
  385.9 2.5 collective-permute-start.2
  388.5 6.0 %collective-permute-done.2 = bf16[512,512]{0,1:T(8,128)(2,1)S(1)} collective-permute-done((bf16[512,512]{0,1:T(8,128)(2,1)S(1)}, bf16[512,512]{0,1:T(8,128)(2,1)S(1)}, u32[]{:S(2)}, u32[]{:S(2)}) %collective-permute-start.2) | collective-permute-done | bytes 524320 | tf_op jit(solution)/shard_map/ppermute | solution.py:116
  394.5 2.5 collective-permute-start.4
  396.9 2.2 broadcast_in_dim.52
  400.0 1.3 collective-permute-start.5
  402.2 0.9 collective-permute-done.4
  403.1 2.5 collective-permute-start.6
  409.8 1.9 collective-permute-done.6
  412.5 52.1 %all-gather.14.cloned.1.call-done = bf16[4096,768]{1,0:T(8,128)(2,1)} async-done(((bf16[128,768]{1,0:T(8,128)(2,1)}), bf16[4096,768]{1,0:T(8,128)(2,1)}) %all-gather.14.cloned.1.call-update) | async-done | bytes 6291472 | tf_op jit(solution)/shard_map/all_gather | solution.py:128
  464.6 8.4 %convolution_convert_fusion = bf16[512,768]{1,0:T(8,128)(2,1)} fusion(bf16[512,4096]{0,1:T(8,128)(2,1)} %constant_dynamic-update-slice_fusion, bf16[4096,768]{1,0:T(8,128)(2,1)} %all-gather.14.cloned.1.call-done), kind=kOutput, calls=%fused_computation.12 | convolution fusion | flops 3221618688 | bytes 11272192 | tf_op jit(solution)/shard_map/dot_general | solution.py:126
  (40 shorter events, 13.1 us)
Async XLA Ops:
  6.5 95.6 %all-gather.8.cloned.1.call-start = ((), (), s32[]{:S(2)}) async-start(), calls=%async_computation | async-start | bytes 6488064 | tf_op jit(solution)/shard_map/all_gather | solution.py:71
  7.3 183.1 %all-gather.12.cloned.1.call-start = ((), (), s32[]{:S(2)}) async-start(), calls=%async_computation.2 | async-start | bytes 6488064 | tf_op jit(solution)/shard_map/all_gather | solution.py:70
  8.0 270.7 %all-gather.10.cloned.1.call-start = ((), (), s32[]{:S(2)}) async-start(), calls=%async_computation.1 | async-start | bytes 6488064 | tf_op jit(solution)/shard_map/all_gather | solution.py:69
  8.7 367.6 %all-gather.16.cloned.1.call-start = ((), (), s32[]{:S(2)}) async-start(), calls=%async_computation.4 | async-start | bytes 8650752 | tf_op jit(solution)/shard_map/all_gather | solution.py:12
  200.0 264.7 %all-gather.14.cloned.1.call-start = ((), (), s32[]{:S(2)}) async-start(), calls=%async_computation.3 | async-start | bytes 6488064 | tf_op jit(solution)/shard_map/all_gather | solution.py:128
  292.4 85.0 %copy-start = (f32[512]{0:T(512)S(1)}, f32[512]{0:T(512)}, u32[]{:S(2)}) copy-start(f32[512]{0:T(512)} %param.16) | copy-start | bytes 6148
  377.5 8.3 %collective-permute-start = (bf16[512,512]{0,1:T(8,128)(2,1)S(1)}, bf16[512,512]{0,1:T(8,128)(2,1)S(1)}, u32[]{:S(2)}, u32[]{:S(2)}) collective-permute-start(bf16[512,512]{0,1:T(8,128)(2,1)S(1)} %bitcast.61), channel_id=1, source_target_pairs={{0,1},{1,2},{2,3},{3,4},{4,5},{5,6},{6,7},{7,0},{8,9},{9,10},{10,1... | collective-permute-start | bytes 1572872 | tf_op jit(solution)/shard_map/ppermute | solution.py:116
  379.7 8.6 %collective-permute-start.1 = (bf16[512,512]{0,1:T(8,128)(2,1)S(1)}, bf16[512,512]{0,1:T(8,128)(2,1)S(1)}, u32[]{:S(2)}, u32[]{:S(2)}) collective-permute-start(bf16[512,512]{0,1:T(8,128)(2,1)S(1)} %bitcast.62), channel_id=1, source_target_pairs={{0,7},{1,0},{2,1},{3,2},{4,3},{5,4},{6,5},{7,6},{8,15},{9,8},{10,9... | collective-permute-start | bytes 1572872 | tf_op jit(solution)/shard_map/ppermute | solution.py:121
  385.9 8.6 %collective-permute-start.2 = (bf16[512,512]{0,1:T(8,128)(2,1)S(1)}, bf16[512,512]{0,1:T(8,128)(2,1)S(1)}, u32[]{:S(2)}, u32[]{:S(2)}) collective-permute-start(bf16[512,512]{0,1:T(8,128)(2,1)S(1)} %collective-permute-done), channel_id=1, source_target_pairs={{0,1},{1,2},{2,3},{3,4},{4,5},{5,6},{6,7},{7,0},{8,9},{9,10},{10,1... | collective-permute-start | bytes 1572872 | tf_op jit(solution)/shard_map/ppermute | solution.py:116
  388.3 11.7 %collective-permute-start.3 = (bf16[512,512]{0,1:T(8,128)(2,1)S(1)}, bf16[512,512]{0,1:T(8,128)(2,1)S(1)}, u32[]{:S(2)}, u32[]{:S(2)}) collective-permute-start(bf16[512,512]{0,1:T(8,128)(2,1)S(1)} %collective-permute-done.1), channel_id=1, source_target_pairs={{0,7},{1,0},{2,1},{3,2},{4,3},{5,4},{6,5},{7,6},{8,15},{9,8},{10,9... | collective-permute-start | bytes 1572872 | tf_op jit(solution)/shard_map/ppermute | solution.py:121
  394.5 8.6 %collective-permute-start.4 = (bf16[512,512]{0,1:T(8,128)(2,1)S(1)}, bf16[512,512]{0,1:T(8,128)(2,1)S(1)}, u32[]{:S(2)}, u32[]{:S(2)}) collective-permute-start(bf16[512,512]{0,1:T(8,128)(2,1)S(1)} %collective-permute-done.2), channel_id=1, source_target_pairs={{0,1},{1,2},{2,3},{3,4},{4,5},{5,6},{6,7},{7,0},{8,9},{9,10},{10,1... | collective-permute-start | bytes 1572872 | tf_op jit(solution)/shard_map/ppermute | solution.py:116
  400.0 9.0 %collective-permute-start.5 = (bf16[512,512]{0,1:T(8,128)(2,1)S(1)}, bf16[512,512]{0,1:T(8,128)(2,1)S(1)}, u32[]{:S(2)}, u32[]{:S(2)}) collective-permute-start(bf16[512,512]{0,1:T(8,128)(2,1)S(1)} %collective-permute-done.3), channel_id=1, source_target_pairs={{0,7},{1,0},{2,1},{3,2},{4,3},{5,4},{6,5},{7,6},{8,15},{9,8},{10,9... | collective-permute-start | bytes 1572872 | tf_op jit(solution)/shard_map/ppermute | solution.py:121
  403.1 8.6 %collective-permute-start.6 = (bf16[512,512]{0,1:T(8,128)(2,1)S(1)}, bf16[512,512]{0,1:T(8,128)(2,1)S(1)}, u32[]{:S(2)}, u32[]{:S(2)}) collective-permute-start(bf16[512,512]{0,1:T(8,128)(2,1)S(1)} %collective-permute-done.4), channel_id=1, source_target_pairs={{0,1},{1,2},{2,3},{3,4},{4,5},{5,6},{6,7},{7,0},{8,9},{9,10},{10,1... | collective-permute-start | bytes 1572872 | tf_op jit(solution)/shard_map/ppermute | solution.py:116
Sparse Core Ops, SparseCore 0:
  9.9 92.1 all-gather.7
  104.7 85.6 all-gather.11
  192.9 85.6 all-gather.9
  281.1 95.1 all-gather.15
  378.8 85.8 all-gather.13
